TPU v7x, 128 devices: a whole 4x4x4 slice. The times are simulated.
128 devices in a mesh: scan: 16 (over z_lo, x, core), tgt: 8 (over y, z_hi).
Axes of the slice: x: 4, y: 4, z: 4 (z_hi: 2, z_lo: 2; z = z_hi * 2 + z_lo), core: 2. Of those that a mesh axis runs over, the one named last changes fastest.
Arguments:
- series: bfloat16 [96, 1200, 8192], P('scan', None, 'tgt'), as said below
- seed_index: int32 [512], replicated, may hold values from 0 to 8191
Outputs:
- affinity: bfloat16 [8192, 8192], P('tgt', 'scan')
Inputs may be any that keep to these rules, and one draw needn't show every extreme that they name: No grayordinate's series is constant over the frames of a scan.
All inputs are finite; a program needn't handle non-finite values.
Results may differ from a plain program's by a relative error of at most 0.0034.
Values may be sent and summed in bfloat16 or wider, within the bound.
A program may use at most 128 MiB of HBM per device.

v0:
```python
import jax
import jax.numpy as jnp
from jax import lax
from jax.sharding import PartitionSpec as P

epsilon = 1e-06
clip_level = 0.95


def fisher_map(values):
    clipped = jnp.clip(values, -clip_level, clip_level)
    return 0.5 * jnp.log((1.0 + clipped) / (1.0 - clipped))


def normalize_columns(profile):
    center = jnp.mean(profile, axis=0)
    deviate = profile - center
    spread = jnp.mean(deviate * deviate, axis=0)
    return (deviate * lax.rsqrt(spread + epsilon)).astype(jnp.bfloat16)


def body(series, seed_index):
    frame_count = series.shape[1]
    local_width = series.shape[2]
    seed_count = seed_index.shape[0]
    tgt_size = lax.axis_size("tgt")
    scan_size = lax.axis_size("scan")
    whole_width = local_width * tgt_size
    first_col = lax.axis_index("tgt") * local_width
    local_seed = seed_index - first_col
    inside = (local_seed >= 0) & (local_seed < local_width)
    safe_seed = jnp.clip(local_seed, 0, local_width - 1)
    values = series.astype(jnp.float32)
    center = jnp.mean(values, axis=1, keepdims=True)
    deviate = values - center
    spread = jnp.mean(deviate * deviate, axis=1, keepdims=True)
    standard = (deviate * lax.rsqrt(spread + epsilon)).astype(jnp.bfloat16)
    picked = jnp.take(standard, safe_seed, axis=2)
    picked = jnp.where(inside[None, None, :], picked, jnp.zeros_like(picked))
    seed_cols = lax.psum(picked, "tgt").astype(jnp.float32).astype(jnp.bfloat16)
    correl = (
        jnp.einsum("sfk,sfg->skg", seed_cols, standard, preferred_element_type=jnp.float32)
        / frame_count
    )
    running = jnp.sum(fisher_map(correl), axis=0)
    total = lax.psum(running, "scan")
    row_prof = normalize_columns(total)
    all_prof = lax.all_gather(row_prof, "tgt", axis=1, tiled=True)
    col_width = whole_width // scan_size
    col_prof = lax.dynamic_slice_in_dim(all_prof, lax.axis_index("scan") * col_width, col_width, 1)
    product = jnp.dot(row_prof.T, col_prof, preferred_element_type=jnp.float32)
    return jnp.tanh(product / seed_count).astype(jnp.bfloat16)


def solution(mesh):
    in_specs = (P("scan", None, "tgt"), P())
    out_specs = P("tgt", "scan")
    return jax.shard_map(body, mesh=mesh, in_specs=in_specs, out_specs=out_specs, check_vma=False)
```

profile of v0, /device:TPU:0, one launch (start us, length us, event | category | flops | bytes accessed | tf_op | source)
XLA Modules:
  0.0 716.1 jit_solution(13805646705477381361)
XLA Ops:
  6.5 0.0 all-reduce.3.cloned.1.call-start
  6.5 0.7 compare_and_fusion
  7.2 28.1 %copy.6 = bf16[6,1200,1024]{1,0,2:T(8,128)(2,1)} copy(bf16[6,1200,1024]{2,1,0:T(8,128)(2,1)} %param.2) | data formatting | bytes 29491200 | tf_op args[0]
  35.4 0.0 copy-start
  35.4 29.1 %convert_reduce_fusion = f32[6,1024]{0,1:T(8,128)S(1)} fusion(bf16[6,1200,1024]{1,0,2:T(8,128)(2,1)} %copy.6), kind=kLoop, calls=%fused_computation.2 | loop fusion | flops 14739456 | bytes 14770176 | tf_op jit(solution)/shard_map/reduce_sum | solution.py:34
  64.6 0.0 copy-done
  64.6 14.9 %fusion.2 = f32[6,1024]{0,1:T(8,128)S(1)} fusion(bf16[6,1200,1024]{1,0,2:T(8,128)(2,1)S(1)} %copy-done, f32[6,1024]{0,1:T(8,128)S(1)} %broadcast_multiply_fusion), kind=kLoop, calls=%fused_computation.5 | loop fusion | flops 29485056 | bytes 14794752 | tf_op jit(solution)/shard_map/reduce_sum | solution.py:36
  79.5 0.1 add_rsqrt_fusion
  79.6 10.1 %fusion.3 = bf16[6,1200,1024]{1,0,2:T(8,128)(2,1)} fusion(bf16[6,1200,1024]{1,0,2:T(8,128)(2,1)S(1)} %copy-done, f32[6,1024]{0,1:T(8,128)S(1)} %add_rsqrt_fusion, f32[6,1024]{0,1:T(8,128)S(1)} %broadcast_multiply_fusion), kind=kLoop, calls=%fused_computation.6 | loop fusion | flops 29491200 | bytes 29540352 | tf_op jit(solution)/shard_map/convert_element_type | solution.py:37
  89.7 21.0 %gather_fusion = bf16[512,6,1200]{2,1,0:T(8,128)(2,1)} fusion(bf16[6,1200,1024]{1,0,2:T(8,128)(2,1)} %fusion.3, s32[1024]{0:T(1024)S(1)} %pad_clamp_fusion), kind=kCustom, calls=%fused_computation | custom fusion | bytes 14747648 | tf_op jit(solution)/shard_map/jit(_take)/gather | solution.py:38
  110.7 14.7 %copy.7 = bf16[512,6,1200]{0,2,1:T(8,128)(2,1)} copy(bf16[512,6,1200]{2,1,0:T(8,128)(2,1)} %gather_fusion) | data formatting | bytes 14745600 | tf_op jit(solution)/shard_map/jit(_take)/gather | solution.py:38
  125.4 6.9 select_bitcast_fusion
  132.3 0.0 all-reduce.3.cloned.1.call-update
  132.3 0.2 all-reduce.5.cloned.1.call-start
  132.6 307.4 %all-reduce.3.cloned.1.call-done = bf16[6,1200,512]{2,1,0:T(8,128)(2,1)} async-done(((bf16[6,1200,512]{2,1,0:T(8,128)(2,1)}), bf16[6,1200,512]{2,1,0:T(8,128)(2,1)}) %all-reduce.3.cloned.1.call-update) | async-done | bytes 7372816 | tf_op jit(solution)/shard_map/psum | solution.py:40
  440.0 22.3 %multiply_reduce_fusion = f32[512,1024]{1,0:T(8,128)} fusion(bf16[6,1200,512]{2,1,0:T(8,128)(2,1)} %all-reduce.3.cloned.1.call-done, bf16[6,1200,1024]{1,0,2:T(8,128)(2,1)} %fusion.3), kind=kOutput, calls=%fused_computation.9 | convolution fusion | flops 7571243008 | bytes 24215552 | tf_op jit(solution)/shard_map/sfk,sfg->skg/dot_general | solution.py:42
  462.3 0.0 all-reduce.5.cloned.1.call-update
  462.4 0.0 all-gather.2.cloned.1.call-start
  462.4 127.5 %all-reduce.5.cloned.1.call-done = f32[512,1024]{1,0:T(8,128)} async-done(((f32[512,1024]{1,0:T(8,128)}), f32[512,1024]{1,0:T(8,128)}) %all-reduce.5.cloned.1.call-update) | async-done | bytes 2097168 | tf_op jit(solution)/shard_map/psum | solution.py:46
  589.9 1.7 reduce_sum.48
  591.6 1.8 multiply_reduce_fusion.1
  593.5 2.9 multiply_convert_fusion
  596.4 0.0 all-gather.2.cloned.1.call-update
  596.5 110.0 %all-gather.2.cloned.1.call-done = bf16[512,8192]{1,0:T(8,128)(2,1)} async-done(((bf16[512,1024]{1,0:T(8,128)(2,1)}), bf16[512,8192]{1,0:T(8,128)(2,1)}) %all-gather.2.cloned.1.call-update) | async-done | bytes 8388624 | tf_op jit(solution)/shard_map/all_gather | solution.py:48
  706.5 3.1 tanh_convert_fusion
  (4 shorter events, 0.1 us)
Async XLA Ops:
  6.5 433.5 %all-reduce.3.cloned.1.call-start = ((), (), s32[]{:S(2)}) async-start(), calls=%async_computation | async-start | bytes 14745600 | tf_op jit(solution)/shard_map/psum | solution.py:40
  35.4 29.2 %copy-start = (bf16[6,1200,1024]{1,0,2:T(8,128)(2,1)S(1)}, bf16[6,1200,1024]{1,0,2:T(8,128)(2,1)}, u32[]{:S(2)}) copy-start(bf16[6,1200,1024]{1,0,2:T(8,128)(2,1)} %copy.6) | copy-start | bytes 44236804
  132.3 457.5 %all-reduce.5.cloned.1.call-start = ((), (), s32[]{:S(2)}) async-start(), calls=%async_computation.1 | async-start | bytes 4194304 | tf_op jit(solution)/shard_map/psum | solution.py:46
  462.4 244.1 %all-gather.2.cloned.1.call-start = ((), (), s32[]{:S(2)}) async-start(), calls=%async_computation.2 | async-start | bytes 9437184 | tf_op jit(solution)/shard_map/all_gather | solution.py:48
Sparse Core Ops, SparseCore 0:
  132.5 307.5 all-reduce.2
  462.5 127.3 all-reduce.4
  596.6 109.8 all-gather.1
where the time goes:
time: 718 us; the launch traced here: 716 us
  waiting for transfers between devices  545 us (76%)
  other arithmetic  68.4 us (10%)
  local copies, waits for them, and re-layouts  63.8 us (9%)
  matrix products  25.4 us (4%)
  between operations  13.2 us (2%)
    psum x1, waiting for transfers between devices, body(): seed_cols = lax.psum(picked, 'tgt').astype(jnp.float32).astype(jnp.bfloat16)  307 us
    psum x1, waiting for transfers between devices, body(): total = lax.psum(running, 'scan')  127 us
    all_gather x1, waiting for transfers between devices, body(): all_prof = lax.all_gather(row_prof, 'tgt', axis=1, tiled=True)  110 us
    gather x2, local copies, waits for them, and re-layouts, body(): picked = jnp.take(standard, safe_seed, axis=2)  35.7 us
    reduce_sum x1, other arithmetic, body(): center = jnp.mean(values, axis=1, keepdims=True)  29.1 us
    unnamed x3, local copies, waits for them, and re-layouts  28.2 us
    dot_general x1, matrix products, body(): jnp.einsum('sfk,sfg->skg', seed_cols, standard, preferred_element_type=jn...  22.3 us
    reduce_sum x1, other arithmetic, body(): spread = jnp.mean(deviate * deviate, axis=1, keepdims=True)  14.9 us
  transfers between devices with their start and end apart: 3, of which 3 were waited for; matrix products, arithmetic and copies ran while one was open for 0% of the time, Pallas kernels for 0%

commit v1 on v0

v1 whole, which is shorter than its diff:
```python
import jax
import jax.numpy as jnp
from jax import lax
from jax.sharding import PartitionSpec as P

epsilon = 1e-06
clip_level = 0.95
capacity = 96


def fisher_sum(correl):
    clipped = jnp.clip(correl, -clip_level, clip_level)
    above = jnp.prod(1.0 + clipped, axis=0)
    below = jnp.prod(1.0 - clipped, axis=0)
    return 0.5 * jnp.log(above / below)


def normalize_columns(profile):
    center = jnp.mean(profile, axis=0)
    deviate = profile - center
    spread = jnp.mean(deviate * deviate, axis=0)
    return (deviate * lax.rsqrt(spread + epsilon)).astype(jnp.bfloat16)


def body(series, seed_index):
    frame_count = series.shape[1]
    local_width = series.shape[2]
    seed_count = seed_index.shape[0]
    tgt_size = lax.axis_size("tgt")
    scan_size = lax.axis_size("scan")
    whole_width = local_width * tgt_size
    me = lax.axis_index("tgt")
    owner = seed_index // local_width
    local_seed = seed_index - owner * local_width
    owned = owner[:, None] == jnp.arange(tgt_size)[None, :]
    before = jnp.cumsum(owned.astype(jnp.int32), axis=0)
    count = before[-1]
    rank = jnp.sum(jnp.where(owned, before, 0), axis=1) - 1

    values = series.astype(jnp.float32)
    center = jnp.mean(values, axis=1, keepdims=True)
    deviate = values - center
    spread = jnp.mean(deviate * deviate, axis=1, keepdims=True)
    standard = (deviate * lax.rsqrt(spread + epsilon)).astype(jnp.bfloat16)

    def correlate(seed_cols):
        correl = jnp.einsum(
            "sfk,sfg->skg", seed_cols, standard, preferred_element_type=jnp.float32
        )
        return fisher_sum(correl / frame_count)

    def packed():
        mine = (owner == me)[:, None] & (rank[:, None] == jnp.arange(capacity)[None, :])
        column = jnp.sum(jnp.where(mine, local_seed[:, None] + 1, 0), axis=0) - 1
        pick = (jnp.arange(local_width)[:, None] == column[None, :]).astype(jnp.bfloat16)
        picked = jnp.einsum(
            "sfg,gk->sfk", standard, pick, preferred_element_type=jnp.float32
        ).astype(jnp.bfloat16)
        seed_cols = lax.all_gather(picked, "tgt", axis=2, tiled=True)
        return jnp.take(correlate(seed_cols), owner * capacity + rank, axis=0)

    def general():
        inside = owner == me
        picked = jnp.take(standard, local_seed, axis=2)
        picked = jnp.where(inside[None, None, :], picked, jnp.zeros_like(picked))
        return correlate(lax.psum(picked, "tgt"))

    running = lax.cond(jnp.max(count) <= capacity, packed, general)
    part = lax.psum_scatter(running, "scan", scatter_dimension=1, tiled=True)
    row_prof = lax.all_gather(normalize_columns(part), "scan", axis=1, tiled=True)
    col_width = whole_width // scan_size
    spot = lax.axis_index("scan") * col_width
    start = spot % local_width
    col_prof = lax.dynamic_slice_in_dim(row_prof, start, col_width, 1)
    col_prof = jnp.where(spot // local_width == me, col_prof, jnp.zeros_like(col_prof))
    col_prof = lax.psum(col_prof, "tgt")
    product = jnp.dot(row_prof.T, col_prof, preferred_element_type=jnp.float32)
    return jnp.tanh(product / seed_count).astype(jnp.bfloat16)


def solution(mesh):
    in_specs = (P("scan", None, "tgt"), P())
    out_specs = P("tgt", "scan")
    return jax.shard_map(body, mesh=mesh, in_specs=in_specs, out_specs=out_specs, check_vma=False)
```

time: 718 us -> 424 us (0.59)
  waiting for transfers between devices: 545 us -> 322 us
  local copies, waits for them, and re-layouts: 63.8 us -> 4.82 us
  other arithmetic: 68.4 us -> 43.5 us
  matrix products: 25.4 us -> 37.4 us
    psum x2 -> x1, waiting for transfers between devices: 435 us -> 86.1 us  [body(): col_prof = lax.psum(col_prof, 'tgt')]
    all_gather x1 -> x2, waiting for transfers between devices: 110 us -> 174 us  [the longest x1 143 us: packed(): seed_cols = lax.all_gather(picked, 'tgt', axis=2, tiled=True)]
    unnamed x3 -> x4, waiting for transfers between devices: 0.05 us -> 61.9 us
    gather x2 -> x1, local copies, waits for them, and re-layouts: 35.7 us -> 2.72 us  [packed(): return jnp.take(correlate(seed_cols), owner * capacity + rank, axis=0)]
    unnamed x3 -> x1, local copies, waits for them, and re-layouts: 28.2 us -> 1.88 us
    reduce_sum x1, other arithmetic: 29.1 us -> 8.78 us  [body(): center = jnp.mean(values, axis=1, keepdims=True)]
    dot_general x1 -> x2, matrix products: 22.3 us -> 34.3 us  [the longest x1 23.5 us: correlate(): jnp.einsum('sfk,sfg->skg', seed_cols, standard, preferred_element_type=jn...]
  transfers between devices with their start and end apart: 3 -> 4, of which waited for: 3 -> 4; matrix products, arithmetic and copies ran while one was open for 0% -> 0% of each run, Pallas kernels for 0% -> 0%
where the time goes in v1:
time: 424 us
  waiting for transfers between devices  322 us (76%)
  other arithmetic  43.5 us (10%)
  matrix products  37.4 us (9%)
  between operations  15.8 us (4%)
  local copies, waits for them, and re-layouts  4.82 us (1%)
    all_gather x1, waiting for transfers between devices, packed(): seed_cols = lax.all_gather(picked, 'tgt', axis=2, tiled=True)  143 us
    psum x1, waiting for transfers between devices, body(): col_prof = lax.psum(col_prof, 'tgt')  86.1 us
    unnamed x4, waiting for transfers between devices  61.9 us
    all_gather x1, waiting for transfers between devices, body(): lax.all_gather(normalize_columns(part), 'scan', axis=1, tiled=True)  31.1 us
    dot_general x1, matrix products, correlate(): jnp.einsum('sfk,sfg->skg', seed_cols, standard, preferred_element_type=jn...  23.5 us
    convert_element_type x1, other arithmetic, body(): standard = (deviate * lax.rsqrt(spread + epsilon)).astype(jnp.bfloat16)  11.7 us
    dot_general x1, matrix products, packed(): jnp.einsum('sfg,gk->sfk', standard, pick, preferred_element_type=jnp.floa...  10.8 us
    reduce_sum x1, other arithmetic, body(): spread = jnp.mean(deviate * deviate, axis=1, keepdims=True)  9.04 us
  transfers between devices with their start and end apart: 4, of which 4 were waited for; matrix products, arithmetic and copies ran while one was open for 0% of the time, Pallas kernels for 0%

profile of v1, /device:TPU:0, one launch (start us, length us, event | category | flops | bytes accessed | tf_op | source)
XLA Modules:
  0.0 424.0 jit_solution(14349586945426796302)
XLA Ops:
  7.4 0.7 multiply_subtract_fusion
  8.1 1.1 reduce-window.6
  9.2 0.2 slice_reduce_fusion
  9.5 0.1 add_bitcast_fusion
  9.5 8.8 %convert_reduce_fusion = f32[6,1024]{1,0:T(8,128)S(1)} fusion(bf16[6,1200,1024]{2,1,0:T(8,128)(2,1)} %param.4), kind=kLoop, calls=%fused_computation.32 | loop fusion | flops 14739456 | bytes 14770176 | tf_op jit(solution)/shard_map/reduce_sum | solution.py:41
  18.3 9.0 %fusion.7 = f32[6,1024]{1,0:T(8,128)S(1)} fusion(bf16[6,1200,1024]{2,1,0:T(8,128)(2,1)} %param.4, f32[6,1024]{1,0:T(8,128)S(1)} %broadcast_multiply_fusion), kind=kLoop, calls=%fused_computation.35 | loop fusion | flops 29485056 | bytes 14794752 | tf_op jit(solution)/shard_map/reduce_sum | solution.py:43
  27.4 11.7 %fusion.8 = bf16[6,1200,1024]{2,1,0:T(8,128)(2,1)} fusion(bf16[6,1200,1024]{2,1,0:T(8,128)(2,1)} %param.4, f32[6,1024]{1,0:T(8,128)S(1)} %add_rsqrt_fusion, f32[6,1024]{1,0:T(8,128)S(1)} %broadcast_multiply_fusion), kind=kLoop, calls=%fused_computation.36 | loop fusion | flops 29491200 | bytes 29540352 | tf_op jit(solution)/shard_map/convert_element_type | solution.py:44
  39.1 0.7 slice_reduce_fusion.1
  40.5 185.9 %conditional.1 = (f32[512,1024]{1,0:T(8,128)S(1)}) conditional(s32[]{:T(128)} %convert_element_type.28, (s32[]{:T(128)}, s32[512]{0:T(512)S(1)}, s32[512]{0:T(512)S(1)}, bf16[6,1200,1024]{2,1,0:T(8,128)(2,1)}) %tuple.11, (s32[512]{0:T(512)S(1)}, s32[512,8]{0,1:T(8,128)S(1)}, s32[512,8]{0,1:T(8,128)S(1)}, s32[512]{0:T(512)S(1)}, s32[]{:T(128)}, ...), branch_computations={%region_5.9_spmd, %region_9.14_spmd} | conditional | flops 12770038784 | bytes 150587424 | solution.py:68
  40.7 0.0 all-gather.3.cloned.1.call-start
  40.8 0.1 select_reduce_fusion
  41.0 10.8 %fusion = bf16[6,1200,96]{1,2,0:T(8,128)(2,1)} fusion(bf16[6,1200,1024]{2,1,0:T(8,128)(2,1)} %get-tuple-element.49, s32[96]{0:T(128)S(1)} %broadcast_add_fusion.1), kind=kOutput, calls=%fused_computation.16 | convolution fusion | flops 1416367104 | bytes 16128384 | tf_op jit(solution)/shard_map/cond/branch_1_fun/sfg,gk->sfk/dot_general | solution.py:56
  51.9 142.9 %all-gather.3.cloned.1.call-done = bf16[6,1200,768]{1,2,0:T(8,128)(2,1)} async-done(((bf16[6,1200,96]{1,2,0:T(8,128)(2,1)}), bf16[6,1200,768]{1,2,0:T(8,128)(2,1)}) %all-gather.3.cloned.1.call-update) | async-done | bytes 11059216 | tf_op jit(solution)/shard_map/cond/branch_1_fun/all_gather | solution.py:59
  194.7 23.5 %subtract_reduce_fusion.1 = (f32[768,1024]{1,0:T(8,128)}, f32[768,1024]{1,0:T(8,128)}) fusion(bf16[6,1200,768]{1,2,0:T(8,128)(2,1)} %all-gather.3.cloned.1.call-done, bf16[6,1200,1024]{2,1,0:T(8,128)(2,1)} %get-tuple-element.49), kind=kOutput, calls=%fused_computation.11 | convolution fusion | flops 11351359488 | bytes 32096256 | tf_op jit(solution)/shard_map/cond/branch_1_fun/sfk,sfg->skg/dot_general | solution.py:47
  218.2 3.7 log_multiply_fusion.1
  221.9 2.7 gather_fusion.1
  224.6 1.8 broadcast_select_fusion
  226.4 0.0 reduce-scatter.4.cloned.1.call-start
  226.4 1.9 copy.18
  228.3 0.0 reduce-scatter.4.cloned.1.call-update
  228.3 0.0 all-gather.5.cloned.1.call-start
  228.4 61.9 %reduce-scatter.4.cloned.1.call-done = f32[64,512]{1,0:T(8,128)} async-done(((f32[1024,512]{1,0:T(8,128)}), f32[64,512]{1,0:T(8,128)}) %reduce-scatter.4.cloned.1.call-update) | async-done | bytes 131088
  290.3 1.0 bitcast_reduce_fusion
  291.3 1.1 multiply_reduce_fusion
  292.4 1.6 multiply_convert_fusion
  294.0 0.0 all-gather.5.cloned.1.call-update
  294.1 0.0 all-reduce.5.cloned.1.call-start
  294.1 31.1 %all-gather.5.cloned.1.call-done = bf16[512,1024]{0,1:T(8,128)(2,1)} async-done(((bf16[512,64]{0,1:T(8,128)(2,1)}), bf16[512,1024]{0,1:T(8,128)(2,1)}) %all-gather.5.cloned.1.call-update) | async-done | bytes 1048592 | tf_op jit(solution)/shard_map/all_gather | solution.py:70
  325.2 1.9 dynamic-slice_select_fusion
  327.2 0.0 all-reduce.5.cloned.1.call-update
  327.2 86.1 %all-reduce.5.cloned.1.call-done = bf16[512,512]{0,1:T(8,128)(2,1)} async-done(((bf16[512,512]{0,1:T(8,128)(2,1)}), bf16[512,512]{0,1:T(8,128)(2,1)}) %all-reduce.5.cloned.1.call-update) | async-done | bytes 524304 | tf_op jit(solution)/shard_map/psum | solution.py:76
  413.3 3.1 tanh_convert_fusion
  (15 shorter events, 0.1 us)
Async XLA Ops:
  40.7 154.0 %all-gather.3.cloned.1.call-start = ((), (), s32[]{:S(2)}) async-start(), calls=%async_computation.2 | async-start | bytes 13271040 | tf_op jit(solution)/shard_map/cond/branch_1_fun/all_gather | solution.py:59
  226.4 63.9 %reduce-scatter.4.cloned.1.call-start = ((), (), s32[]{:S(2)}) async-start(), calls=%async_computation.5 | async-start | bytes 2228224
  228.3 96.9 %all-gather.5.cloned.1.call-start = ((), (), s32[]{:S(2)}) async-start(), calls=%async_computation.3 | async-start | bytes 1114112 | tf_op jit(solution)/shard_map/all_gather | solution.py:70
  294.1 119.2 %all-reduce.5.cloned.1.call-start = ((), (), s32[]{:S(2)}) async-start(), calls=%async_computation.4 | async-start | bytes 1048576 | tf_op jit(solution)/shard_map/psum | solution.py:76
Sparse Core Ops, SparseCore 0:
  52.0 142.6 all-gather.2
Sparse Core Ops, SparseCore 1:
  229.2 61.0 reduce-scatter.3
  294.1 31.0 all-gather.4
  327.6 85.7 all-reduce.4

commit v2 on v1

v2 whole, which is shorter than its diff:
```python
import functools

import jax
import jax.numpy as jnp
from jax import lax
from jax.experimental import pallas as pl
from jax.experimental.pallas import tpu as pltpu
from jax.sharding import PartitionSpec as P

epsilon = 1e-06
clip_level = 0.95
capacities = (80, 96)
MESH = pl.DeviceIdType.MESH

place_table = ((0, 2, 5, 1), (3, 6, 7, 4))


def fisher_sum(correl):
    clipped = jnp.clip(correl, -clip_level, clip_level)
    above = jnp.prod(1.0 + clipped, axis=0)
    below = jnp.prod(1.0 - clipped, axis=0)
    return 0.5 * jnp.log(above / below)


def normalize_columns(profile):
    center = jnp.mean(profile, axis=0)
    deviate = profile - center
    spread = jnp.mean(deviate * deviate, axis=0)
    return (deviate * lax.rsqrt(spread + epsilon)).astype(jnp.bfloat16)


def profile_kernel(
    cap,
    series_ref,
    pick_ref,
    out_ref,
    raw,
    standard,
    near,
    far,
    above,
    below,
    load_sem,
    send_sem,
    recv_sem,
):
    scans, frames, width = standard.shape
    me = lax.axis_index("scan")
    own = lax.axis_index("tgt")
    step = 2 - 4 * lax.rem(me, 2)
    ahead = (me, lax.rem(own + 8 + step, 8))
    behind = (me, lax.rem(own + 8 - step, 8))
    across = (me, own + 1 - 2 * lax.rem(own, 2))

    def load(s):
        slot = lax.rem(s, 2)
        return pltpu.make_async_copy(series_ref.at[s], raw.at[slot], load_sem.at[slot])

    load(0).start()
    barrier = pltpu.get_barrier_semaphore()
    for peer in (ahead, behind, across):
        pl.semaphore_signal(barrier, inc=1, device_id=peer, device_id_type=MESH)
    pl.semaphore_wait(barrier, 3)

    def rows(block):
        return pl.ds(block * cap, cap)

    flows = (
        (near, 0, near, 1, ahead),
        (near, 0, near, 2, behind),
        (near, 0, near, 3, across),
        (near, 1, far, 0, across),
        (near, 1, far, 1, ahead),
        (near, 3, far, 2, behind),
        (far, 0, far, 3, ahead),
    )

    def flow(f, s):
        source, source_block, target, target_block, peer = flows[f]
        return pltpu.make_async_remote_copy(
            src_ref=source.at[s, rows(source_block)],
            dst_ref=target.at[s, rows(target_block)],
            send_sem=send_sem.at[f, s],
            recv_sem=recv_sem.at[f, s],
            device_id=peer,
            device_id_type=MESH,
        )

    piece = 80
    pieces = frames // piece

    def fold(values):
        return jnp.sum(values.reshape(piece // 8, 8, width), axis=0)

    def standardize(s):
        slot = lax.rem(s, 2)

        def read(r):
            return raw[slot, pl.ds(r * piece, piece), :].astype(jnp.float32)

        zero = jnp.zeros((8, width), jnp.float32)
        total = lax.fori_loop(0, pieces, lambda r, acc: acc + fold(read(r)), zero)
        center = jnp.sum(total, axis=0, keepdims=True) / frames

        def squares(r, acc):
            deviate = read(r) - center
            return acc + fold(deviate * deviate)

        total = lax.fori_loop(0, pieces, squares, zero)
        spread = jnp.sum(total, axis=0, keepdims=True) / frames
        scale = lax.rsqrt(spread + epsilon)

        @pl.loop(0, pieces)
        def _(r):
            standard[s, pl.ds(r * piece, piece), :] = ((read(r) - center) * scale).astype(
                jnp.bfloat16
            )

        picked = lax.dot_general(
            pick_ref[...],
            standard[s],
            (((1,), (1,)), ((), ())),
            preferred_element_type=jnp.float32,
        )
        near[s, 0:cap, :] = picked.astype(jnp.bfloat16)

    chunk = 256

    def correlate(blocks, group, s):
        @pl.loop(0, width // chunk)
        def _(c):
            columns = pl.ds(pl.multiple_of(c * chunk, chunk), chunk)
            correl = jnp.dot(
                blocks[s], standard[s, :, columns], preferred_element_type=jnp.float32
            )
            clipped = jnp.clip(correl * (1.0 / frames), -clip_level, clip_level)
            above[group, :, columns] *= 1.0 + clipped
            below[group, :, columns] *= 1.0 - clipped

    def finish(group):
        @pl.loop(0, 4 * cap // 16)
        def _(r):
            at = pl.ds(r * 16, 16)
            out_ref[pl.ds(group * 4 * cap + r * 16, 16), :] = 0.5 * jnp.log(
                above[group, at, :] / below[group, at, :]
            )

    def body(i, carry):
        @pl.when(i < scans)
        def _():
            load(i).wait()

            @pl.when(i < scans - 1)
            def _():
                load(i + 1).start()

            standardize(i)

            @pl.when(i == 0)
            def _():
                above[...] = jnp.ones_like(above)
                below[...] = jnp.ones_like(below)

        @pl.when((i >= 2) & (i < scans + 2))
        def _():
            flow(0, i - 2).wait_recv()
            flow(3, i - 2).start()
            flow(4, i - 2).start()
            flow(2, i - 2).wait_recv()
            flow(5, i - 2).start()

        @pl.when((i >= 4) & (i < scans + 4))
        def _():
            flow(3, i - 4).wait_recv()
            flow(6, i - 4).start()

        @pl.when(i < scans)
        def _():
            for f in range(3):
                flow(f, i).start()

        @pl.when((i >= 2) & (i < scans + 2))
        def _():
            flow(1, i - 2).wait_recv()
            correlate(near, 0, i - 2)

        @pl.when(i == scans + 2)
        def _():
            finish(0)

        @pl.when(i >= 6)
        def _():
            for f in (4, 5, 6):
                flow(f, i - 6).wait_recv()
            correlate(far, 1, i - 6)

        return carry

    lax.fori_loop(0, scans + 6, body, 0)
    finish(1)

    @pl.loop(0, scans)
    def _(s):
        for f in range(7):
            flow(f, s).wait_send()


def packed_profile(cap, series, pick):
    scans, frames, width = series.shape
    return pl.pallas_call(
        functools.partial(profile_kernel, cap),
        out_shape=jax.ShapeDtypeStruct((8 * cap, width), jnp.float32),
        in_specs=[
            pl.BlockSpec(memory_space=pl.ANY),
            pl.BlockSpec(memory_space=pltpu.VMEM),
        ],
        out_specs=pl.BlockSpec(memory_space=pltpu.VMEM),
        scratch_shapes=[
            pltpu.VMEM((2, frames, width), jnp.bfloat16),
            pltpu.VMEM((scans, frames, width), jnp.bfloat16),
            pltpu.VMEM((scans, 4 * cap, frames), jnp.bfloat16),
            pltpu.VMEM((scans, 4 * cap, frames), jnp.bfloat16),
            pltpu.VMEM((2, 4 * cap, width), jnp.float32),
            pltpu.VMEM((2, 4 * cap, width), jnp.float32),
            pltpu.SemaphoreType.DMA((2,)),
            pltpu.SemaphoreType.DMA((7, scans)),
            pltpu.SemaphoreType.DMA((7, scans)),
        ],
        name="profile_%d" % cap,
        compiler_params=pltpu.CompilerParams(
            collective_id=cap, has_side_effects=True, vmem_limit_bytes=60 * 2**20
        ),
    )(series, pick)


def general_profile(series, owner, local_seed, me):
    frame_count = series.shape[1]
    values = series.astype(jnp.float32)
    center = jnp.mean(values, axis=1, keepdims=True)
    deviate = values - center
    spread = jnp.mean(deviate * deviate, axis=1, keepdims=True)
    standard = (deviate * lax.rsqrt(spread + epsilon)).astype(jnp.bfloat16)
    picked = jnp.take(standard, local_seed, axis=2)
    picked = jnp.where((owner == me)[None, None, :], picked, jnp.zeros_like(picked))
    correl = jnp.einsum(
        "sfk,sfg->skg",
        lax.psum(picked, "tgt"),
        standard,
        preferred_element_type=jnp.float32,
    )
    return fisher_sum(correl / frame_count)


def body(series, seed_index):
    local_width = series.shape[2]
    seed_count = seed_index.shape[0]
    tgt_size = lax.axis_size("tgt")
    scan_size = lax.axis_size("scan")
    whole_width = local_width * tgt_size
    me = lax.axis_index("tgt")
    owner = seed_index // local_width
    local_seed = seed_index - owner * local_width
    owned = owner[:, None] == jnp.arange(tgt_size)[None, :]
    before = jnp.cumsum(owned.astype(jnp.int32), axis=0)
    most = jnp.max(before[-1])
    rank = jnp.sum(jnp.where(owned, before, 0), axis=1) - 1
    sense = 1 - 2 * (lax.axis_index("scan") % 2)
    along = (sense * (owner // 2 - me // 2)) % 4
    place = jnp.asarray(place_table)[(owner + me) % 2, along]

    def packed(cap):
        def branch():
            mine = (owner == me)[None, :] & (
                rank[None, :] == jnp.arange(cap, dtype=jnp.int32)[:, None]
            )
            column = jnp.sum(jnp.where(mine, local_seed[None, :] + 1, 0), axis=1) - 1
            pick = (column[:, None] == jnp.arange(local_width)[None, :]).astype(jnp.bfloat16)
            profile = packed_profile(cap, series, pick)
            return jnp.take(profile, place * cap + rank, axis=0)

        return branch

    branches = [packed(cap) for cap in capacities]
    branches.append(lambda: general_profile(series, owner, local_seed, me))
    choice = sum((most > cap).astype(jnp.int32) for cap in capacities)
    running = lax.switch(choice, branches)
    part = lax.psum_scatter(running, "scan", scatter_dimension=1, tiled=True)
    row_prof = lax.all_gather(normalize_columns(part), "scan", axis=1, tiled=True)
    col_width = whole_width // scan_size
    spot = lax.axis_index("scan") * col_width
    start = spot % local_width
    col_prof = lax.dynamic_slice_in_dim(row_prof, start, col_width, 1)
    col_prof = jnp.where(spot // local_width == me, col_prof, jnp.zeros_like(col_prof))
    col_prof = lax.psum(col_prof, "tgt")
    product = jnp.dot(row_prof.T, col_prof, preferred_element_type=jnp.float32)
    return jnp.tanh(product / seed_count).astype(jnp.bfloat16)


def solution(mesh):
    in_specs = (P("scan", None, "tgt"), P())
    out_specs = P("tgt", "scan")
    return jax.shard_map(body, mesh=mesh, in_specs=in_specs, out_specs=out_specs, check_vma=False)
```

time: 424 us -> 304 us (0.72)
  waiting for transfers between devices: 322 us -> 179 us
  Pallas kernels: 0 us -> 82.2 us
  matrix products: 37.4 us -> 3.07 us
  other arithmetic: 43.5 us -> 10.8 us
  local copies, waits for them, and re-layouts: 4.82 us -> 12.6 us
    all_gather x1 -> x0, waiting for transfers between devices: 143 us -> none  [packed(): seed_cols = lax.all_gather(picked, 'tgt', axis=2, tiled=True)]
    pallas_call x0 -> x1, Pallas kernels: none -> 82.2 us  [packed_profile(): pl.pallas_call(functools.partial(profile_kernel, cap), out_shape=jax.Shap...]
    dot_general x2 -> x0, matrix products: 34.3 us -> none  [the longest x1 23.5 us: correlate(): jnp.einsum('sfk,sfg->skg', seed_cols, standard, preferred_element_type=jn...]
    reduce_sum x3 -> x1, other arithmetic: 17.9 us -> 0.13 us  [branch(): column = jnp.sum(jnp.where(mine, local_seed[None, :] + 1, 0), axis=1) - 1]
    convert_element_type x1, other arithmetic: 11.7 us -> 0.77 us  [branch(): (column[:, None] == jnp.arange(local_width)[None, :]).astype(jnp.bfloat16)]
    gather x1 -> x2, local copies, waits for them, and re-layouts: 2.72 us -> 9.44 us  [the longest x1 4.88 us: body(): place = jnp.asarray(place_table)[(owner + me) % 2, along]]
  transfers between devices with their start and end apart: 4 -> 3, of which waited for: 4 -> 3; matrix products, arithmetic and copies ran while one was open for 0% -> 0% of each run, Pallas kernels for 0% -> 0%
where the time goes in v2:
time: 304 us
  waiting for transfers between devices  179 us (59%)
  Pallas kernels  82.2 us (27%)
  between operations  16.4 us (5%)
  local copies, waits for them, and re-layouts  12.6 us (4%)
  other arithmetic  10.8 us (4%)
  matrix products  3.07 us (1%)
    psum x1, waiting for transfers between devices, body(): col_prof = lax.psum(col_prof, 'tgt')  86.1 us
    pallas_call x1, Pallas kernels, packed_profile(): pl.pallas_call(functools.partial(profile_kernel, cap), out_shape=jax.Shap...  82.2 us
    unnamed x4, waiting for transfers between devices  61.6 us
    all_gather x1, waiting for transfers between devices, body(): lax.all_gather(normalize_columns(part), 'scan', axis=1, tiled=True)  31.1 us
  transfers between devices with their start and end apart: 3, of which 3 were waited for; matrix products, arithmetic and copies ran while one was open for 0% of the time, Pallas kernels for 0%

profile of v2, /device:TPU:0, one launch (start us, length us, event | category | flops | bytes accessed | tf_op | source)
XLA Modules:
  0.0 304.1 jit_solution(8278751282496774881)
XLA Ops:
  7.4 0.7 multiply_subtract_fusion
  8.1 1.1 reduce-window.6
  9.2 0.2 slice_reduce_fusion
  9.5 0.1 add_bitcast_fusion
  9.5 0.7 slice_reduce_fusion.1
  11.6 94.2 %conditional.1 = (f32[512,1024]{1,0:T(8,128)}) conditional(s32[]{:T(128)} %clamp.4, ((), s32[512,2]{0,1:T(2,128)S(1)}, s32[512]{0:T(512)S(1)}, s32[512,8]{0,1:T(8,128)S(1)}, s32[512,8]{0,1:T(8,128)S(1)}, /*index=5*/s32[512]{0:T(512)S(1)}, s32[]{:T(128)}, s32[512]{0:T(512)S(1)}, bf16[6,1200,1024]{2,1,0:T(8,128)(2,1)}) %tuple.14, ((), ...), branch_computations={%region_3.6_spmd, %region_6.9_spmd, %region_9.15_spmd} | conditional | flops 7653421056 | bytes 268773440 | solution.py:286
  11.7 4.9 %gather_fusion = s32[512]{0:T(512)S(1)} fusion(s32[2,4]{1,0:T(2,128)} %constant.207.clone.1, s32[512]{0:T(512)S(1)} %bitcast.22), kind=kCustom, calls=%fused_computation | custom fusion | bytes 8192 | tf_op jit(solution)/shard_map/gather | solution.py:269
  16.6 0.1 select_reduce_fusion
  16.7 0.8 fusion.pick_ref
  17.5 82.2 %profile_80.1 = f32[640,1024]{1,0:T(8,128)} custom-call(bf16[6,1200,1024]{2,1,0:T(8,128)(2,1)} %get-tuple-element.79.series_ref, bf16[80,1024]{1,0:T(8,128)(2,1)} %fusion.pick_ref), custom_call_target="tpu_custom_call" | custom-call | tf_op jit(solution)/shard_map/cond/branch_0_fun/profile_80/pallas_call | solution.py:210
  99.7 4.6 %gather_fusion.1 = f32[512,1024]{1,0:T(8,128)S(1)} fusion(f32[640,1024]{1,0:T(8,128)} %profile_80.1, s32[1024]{0:T(1024)S(1)} %pad_clamp_fusion), kind=kCustom, calls=%fused_computation.1 | custom fusion | bytes 4196352 | tf_op jit(solution)/shard_map/cond/branch_0_fun/jit(_take)/gather | solution.py:279
  104.3 1.5 broadcast_select_fusion
  105.8 0.0 reduce-scatter.4.cloned.1.call-start
  105.8 2.9 copy.21
  108.7 0.0 reduce-scatter.4.cloned.1.call-update
  108.8 0.0 all-gather.2.cloned.1.call-start
  108.8 61.5 %reduce-scatter.4.cloned.1.call-done = f32[64,512]{1,0:T(8,128)} async-done(((f32[1024,512]{1,0:T(8,128)}), f32[64,512]{1,0:T(8,128)}) %reduce-scatter.4.cloned.1.call-update) | async-done | bytes 131088
  170.3 1.0 bitcast_reduce_fusion
  171.4 1.1 multiply_reduce_fusion
  172.5 1.6 multiply_convert_fusion
  174.1 0.0 all-gather.2.cloned.1.call-update
  174.1 0.0 all-reduce.5.cloned.1.call-start
  174.2 31.1 %all-gather.2.cloned.1.call-done = bf16[512,1024]{0,1:T(8,128)(2,1)} async-done(((bf16[512,64]{0,1:T(8,128)(2,1)}), bf16[512,1024]{0,1:T(8,128)(2,1)}) %all-gather.2.cloned.1.call-update) | async-done | bytes 1048592 | tf_op jit(solution)/shard_map/all_gather | solution.py:288
  205.3 1.9 dynamic-slice_select_fusion
  207.3 0.0 all-reduce.5.cloned.1.call-update
  207.3 86.1 %all-reduce.5.cloned.1.call-done = bf16[512,512]{0,1:T(8,128)(2,1)} async-done(((bf16[512,512]{0,1:T(8,128)(2,1)}), bf16[512,512]{0,1:T(8,128)(2,1)}) %all-reduce.5.cloned.1.call-update) | async-done | bytes 524304 | tf_op jit(solution)/shard_map/psum | solution.py:294
  293.4 3.1 %tanh_convert_fusion = bf16[1024,512]{1,0:T(8,128)(2,1)} fusion(bf16[512,1024]{0,1:T(8,128)(2,1)} %all-gather.2.cloned.1.call-done, bf16[512,512]{0,1:T(8,128)(2,1)} %all-reduce.5.cloned.1.call-done), kind=kOutput, calls=%fused_computation.52 | convolution fusion | flops 537919488 | bytes 2621440 | tf_op jit(solution)/shard_map/dot_general | solution.py:295
  (15 shorter events, 0.2 us)
Async XLA Ops:
  105.8 64.5 %reduce-scatter.4.cloned.1.call-start = ((), (), s32[]{:S(2)}) async-start(), calls=%async_computation.4 | async-start | bytes 2228224
  108.8 96.6 %all-gather.2.cloned.1.call-start = ((), (), s32[]{:S(2)}) async-start(), calls=%async_computation.2 | async-start | bytes 1114112 | tf_op jit(solution)/shard_map/all_gather | solution.py:288
  174.1 119.3 %all-reduce.5.cloned.1.call-start = ((), (), s32[]{:S(2)}) async-start(), calls=%async_computation.3 | async-start | bytes 1048576 | tf_op jit(solution)/shard_map/psum | solution.py:294
Sparse Core Ops, SparseCore 1:
  108.8 61.4 reduce-scatter.3
  174.2 31.1 all-gather.1
  207.7 85.7 all-reduce.4

commit v3 on v2

--- a/solution.py
+++ b/solution.py
@@ -20,13 +20,6 @@
     above = jnp.prod(1.0 + clipped, axis=0)
     below = jnp.prod(1.0 - clipped, axis=0)
     return 0.5 * jnp.log(above / below)
-
-
-def normalize_columns(profile):
-    center = jnp.mean(profile, axis=0)
-    deviate = profile - center
-    spread = jnp.mean(deviate * deviate, axis=0)
-    return (deviate * lax.rsqrt(spread + epsilon)).astype(jnp.bfloat16)
 
 
 def profile_kernel(
@@ -233,6 +226,275 @@
     )(series, pick)
 
 
+def spread_kernel(
+    run,
+    row_out,
+    col_out,
+    swap,
+    half,
+    from_z,
+    quarter,
+    from_x,
+    full,
+    row,
+    col,
+    swap_send,
+    swap_recv,
+    z_send,
+    z_recv,
+    x_send,
+    x_recv,
+    join_send,
+    join_recv,
+    piece_send,
+    piece_recv,
+    tree_send,
+    tree_recv,
+):
+    seeds, width = run.shape
+    count = seeds // 2
+    wide = width // 2
+    lane = wide // 4
+    parts = 4
+    me = lax.axis_index("scan")
+    own = lax.axis_index("tgt")
+    core = lax.rem(me, 2)
+    along_x = lax.rem(me // 2, 4)
+    low = me // 8
+
+    def turn(d):
+        return lax.rem(along_x + 4 + d, 4)
+
+    def beside(d):
+        return (low * 8 + turn(d) * 2 + core, own)
+
+    partner = (me + 1 - 2 * core, own)
+    above = (lax.rem(me + 8, 16), own)
+    step = 2 - 4 * core
+    ahead = (me, lax.rem(own + 8 + step, 8))
+    behind = (me, lax.rem(own + 8 - step, 8))
+    across = (me, own + 1 - 2 * lax.rem(own, 2))
+
+    barrier = pltpu.get_barrier_semaphore()
+    for peer in (partner, above, beside(1), beside(2), beside(3), ahead, behind, across):
+        pl.semaphore_signal(barrier, inc=1, device_id=peer, device_id_type=MESH)
+    pl.semaphore_wait(barrier, 8)
+
+    def remote(source, target, send, recv, peer):
+        return pltpu.make_async_remote_copy(
+            src_ref=source,
+            dst_ref=target,
+            send_sem=send,
+            recv_sem=recv,
+            device_id=peer,
+            device_id_type=MESH,
+        )
+
+    size = count // parts
+    mine = pl.multiple_of(core * count, count)
+    other = pl.multiple_of(count - core * count, count)
+
+    def rows(c):
+        return pl.ds(c * size, size)
+
+    def rows_from(base, c):
+        return pl.ds(pl.multiple_of(base + c * size, size), size)
+
+    def lanes(index, length):
+        return pl.ds(pl.multiple_of(index * length, length), length)
+
+    def swap_copy(c):
+        return remote(
+            run.at[rows_from(other, c)], swap.at[rows(c)], swap_send.at[c], swap_recv.at[c], partner
+        )
+
+    def z_copy(c):
+        return remote(
+            half.at[rows(c), lanes(1 - low, wide)],
+            from_z.at[rows(c)],
+            z_send.at[c],
+            z_recv.at[c],
+            above,
+        )
+
+    def x_copy(c, d):
+        return remote(
+            quarter.at[rows(c), lanes(turn(d), lane)],
+            from_x.at[d - 1, rows(c)],
+            x_send.at[d - 1, c],
+            x_recv.at[d - 1, c],
+            beside(d),
+        )
+
+    def join_copy(c):
+        at = rows_from(mine, c)
+        return remote(full.at[at], full.at[at], join_send.at[c], join_recv.at[c], partner)
+
+    for c in range(parts):
+        swap_copy(c).start()
+    for c in range(parts):
+        swap_copy(c).wait_recv()
+        half[rows(c), :] = run[rows_from(mine, c), :] + swap[rows(c), :]
+        z_copy(c).start()
+    for c in range(parts):
+        z_copy(c).wait_recv()
+        quarter[rows(c), :] = half[rows(c), lanes(low, wide)] + from_z[rows(c), :]
+        for d in (1, 3, 2):
+            x_copy(c, d).start()
+    for c in range(parts):
+        for d in (1, 3, 2):
+            x_copy(c, d).wait_recv()
+        near = quarter[rows(c), lanes(along_x, lane)] + from_x[0, rows(c), :]
+        full[rows_from(mine, c), :] = near + (from_x[1, rows(c), :] + from_x[2, rows(c), :])
+        join_copy(c).start()
+    for c in range(parts):
+        join_copy(c).wait_recv()
+
+    profile = full[...]
+    center = jnp.sum(profile, axis=0, keepdims=True) / seeds
+    deviate = profile - center
+    spread = jnp.sum(deviate * deviate, axis=0, keepdims=True) / seeds
+    row[:, lanes(low * 4 + along_x, lane)] = (deviate * lax.rsqrt(spread + epsilon)).astype(
+        jnp.bfloat16
+    )
+
+    def piece_copy(k, index, peer):
+        at = row.at[pl.ds(mine, count), lanes(index, lane)]
+        return remote(at, at, piece_send.at[k], piece_recv.at[k], peer)
+
+    def here(d):
+        return low * 4 + turn(-d)
+
+    def there(d):
+        return (1 - low) * 4 + turn(-d)
+
+    def over_x(d):
+        return piece_copy(d - 1, here(0), beside(d))
+
+    def over_z(d):
+        return piece_copy(3 + d, here(d), above)
+
+    def over_core(k):
+        return piece_copy(7 + k, here(k + 1) if k < 3 else there(k - 3), partner)
+
+    for d in (1, 3, 2):
+        over_x(d).start()
+    over_z(0).start()
+    for d in (1, 3, 2):
+        over_x(d).wait_recv()
+        over_z(d).start()
+        over_core(d - 1).start()
+    for d in (0, 1, 3, 2):
+        over_z(d).wait_recv()
+        over_core(3 + d).start()
+    for k in (0, 2, 1, 3, 4, 6, 5):
+        over_core(k).wait_recv()
+
+    root = me // 2
+    sense = 1 - 2 * core
+    far_y = lax.rem(sense * (own // 2 - root // 2) + 8, 4)
+    same_z = lax.rem(own + root, 2) == 0
+    is_root = (far_y == 0) & same_z
+    sends_on = far_y < 2
+    bulk = seeds // parts
+
+    def tree_copy(kind, c):
+        at = col.at[pl.ds(c * bulk, bulk)]
+        peer = (ahead, behind, across)[kind]
+        return remote(at, at, tree_send.at[kind, c], tree_recv.at[c], peer)
+
+    @pl.when(is_root)
+    def _():
+        col[...] = row[:, lanes(core, wide)]
+
+    for c in range(parts):
+
+        @pl.when(jnp.logical_not(is_root))
+        def _():
+            tree_copy(0, c).wait_recv()
+
+        @pl.when(is_root)
+        def _():
+            tree_copy(2, c).start()
+
+        @pl.when(sends_on)
+        def _():
+            tree_copy(0, c).start()
+
+        @pl.when(far_y == 0)
+        def _():
+            tree_copy(1, c).start()
+
+    row_out[...] = row[...]
+    col_out[...] = col[...]
+
+    for c in range(parts):
+        swap_copy(c).wait_send()
+        z_copy(c).wait_send()
+        for d in (1, 2, 3):
+            x_copy(c, d).wait_send()
+        join_copy(c).wait_send()
+    for d in (1, 2, 3):
+        over_x(d).wait_send()
+    for d in range(4):
+        over_z(d).wait_send()
+    for k in range(7):
+        over_core(k).wait_send()
+    for c in range(parts):
+
+        @pl.when(is_root)
+        def _():
+            tree_copy(2, c).wait_send()
+
+        @pl.when(sends_on)
+        def _():
+            tree_copy(0, c).wait_send()
+
+        @pl.when(far_y == 0)
+        def _():
+            tree_copy(1, c).wait_send()
+
+
+def spread_profiles(running, col_width):
+    seeds, width = running.shape
+    count, wide, lane = seeds // 2, width // 2, width // 8
+    dma = pltpu.SemaphoreType.DMA
+    whole = pl.BlockSpec(memory_space=pltpu.VMEM)
+    return pl.pallas_call(
+        spread_kernel,
+        out_shape=(
+            jax.ShapeDtypeStruct((seeds, width), jnp.bfloat16),
+            jax.ShapeDtypeStruct((seeds, col_width), jnp.bfloat16),
+        ),
+        in_specs=[whole],
+        out_specs=(whole, whole),
+        scratch_shapes=[
+            pltpu.VMEM((count, width), jnp.float32),
+            pltpu.VMEM((count, width), jnp.float32),
+            pltpu.VMEM((count, wide), jnp.float32),
+            pltpu.VMEM((count, wide), jnp.float32),
+            pltpu.VMEM((3, count, lane), jnp.float32),
+            pltpu.VMEM((seeds, lane), jnp.float32),
+            pltpu.VMEM((seeds, width), jnp.bfloat16),
+            pltpu.VMEM((seeds, col_width), jnp.bfloat16),
+            dma((4,)),
+            dma((4,)),
+            dma((4,)),
+            dma((4,)),
+            dma((3, 4)),
+            dma((3, 4)),
+            dma((4,)),
+            dma((4,)),
+            dma((14,)),
+            dma((14,)),
+            dma((3, 4)),
+            dma((4,)),
+        ],
+        name="spread",
+        compiler_params=pltpu.CompilerParams(collective_id=1, has_side_effects=True),
+    )(running)
+
+
 def general_profile(series, owner, local_seed, me):
     frame_count = series.shape[1]
     values = series.astype(jnp.float32)
@@ -284,14 +546,7 @@
     branches.append(lambda: general_profile(series, owner, local_seed, me))
     choice = sum((most > cap).astype(jnp.int32) for cap in capacities)
     running = lax.switch(choice, branches)
-    part = lax.psum_scatter(running, "scan", scatter_dimension=1, tiled=True)
-    row_prof = lax.all_gather(normalize_columns(part), "scan", axis=1, tiled=True)
-    col_width = whole_width // scan_size
-    spot = lax.axis_index("scan") * col_width
-    start = spot % local_width
-    col_prof = lax.dynamic_slice_in_dim(row_prof, start, col_width, 1)
-    col_prof = jnp.where(spot // local_width == me, col_prof, jnp.zeros_like(col_prof))
-    col_prof = lax.psum(col_prof, "tgt")
+    row_prof, col_prof = spread_profiles(running, whole_width // scan_size)
     product = jnp.dot(row_prof.T, col_prof, preferred_element_type=jnp.float32)
     return jnp.tanh(product / seed_count).astype(jnp.bfloat16)
 

time: 304 us -> 173 us (0.57)
  the two profiles are of different devices: /device:TPU:0 before, /device:TPU:19 now
where the time goes in v3:
time: 173 us; the launch traced here: 172 us
  Pallas kernels  140 us (81%)
  between operations  14.7 us (8%)
  local copies, waits for them, and re-layouts  9.66 us (6%)
  other arithmetic  5.21 us (3%)
  matrix products  3.11 us (2%)
    pallas_call x1, Pallas kernels, packed_profile(): pl.pallas_call(functools.partial(profile_kernel, cap), out_shape=jax.Shap...  80.4 us
    pallas_call x1, Pallas kernels, spread_profiles(): pl.pallas_call(spread_kernel, out_shape=(jax.ShapeDtypeStruct((seeds, wid...  59.3 us
    gather x1, local copies, waits for them, and re-layouts, body(): place = jnp.asarray(place_table)[(owner + me) % 2, along]  4.88 us
    gather x1, local copies, waits for them, and re-layouts, branch(): return jnp.take(profile, place * cap + rank, axis=0)  4.56 us

profile of v3, /device:TPU:19, one launch (start us, length us, event | category | flops | bytes accessed | tf_op | source)
XLA Modules:
  0.0 172.4 jit_solution(369675489397425773)
XLA Ops:
  6.5 0.7 multiply_subtract_fusion
  7.3 1.1 reduce-window.6
  8.4 0.2 slice_reduce_fusion
  8.7 0.1 add_bitcast_fusion
  8.8 0.7 slice_reduce_fusion.1
  10.8 92.4 %conditional.1 = (f32[512,1024]{1,0:T(8,128)}) conditional(s32[]{:T(128)} %clamp.4, ((), s32[512,2]{0,1:T(2,128)S(1)}, s32[512]{0:T(512)S(1)}, s32[512,8]{0,1:T(8,128)S(1)}, s32[512,8]{0,1:T(8,128)S(1)}, /*index=5*/s32[512]{0:T(512)S(1)}, s32[]{:T(128)}, s32[512]{0:T(512)S(1)}, bf16[6,1200,1024]{2,1,0:T(8,128)(2,1)}) %tuple.14, ((), ...), branch_computations={%region_3.6_spmd, %region_6.9_spmd, %region_9.15_spmd} | conditional | flops 7653421056 | bytes 268773440 | solution.py:548
  10.8 4.9 %gather_fusion = s32[512]{0:T(512)S(1)} fusion(s32[2,4]{1,0:T(2,128)} %constant.182.clone.1, s32[512]{0:T(512)S(1)} %bitcast.14), kind=kCustom, calls=%fused_computation | custom fusion | bytes 8192 | tf_op jit(solution)/shard_map/gather | solution.py:531
  15.7 0.1 select_reduce_fusion
  15.9 0.8 fusion.pick_ref
  16.6 80.4 %profile_80.1 = f32[640,1024]{1,0:T(8,128)} custom-call(bf16[6,1200,1024]{2,1,0:T(8,128)(2,1)} %get-tuple-element.79.series_ref, bf16[80,1024]{1,0:T(8,128)(2,1)} %fusion.pick_ref), custom_call_target="tpu_custom_call" | custom-call | tf_op jit(solution)/shard_map/cond/branch_0_fun/profile_80/pallas_call | solution.py:203
  97.0 4.6 %gather_fusion.1 = f32[512,1024]{1,0:T(8,128)S(1)} fusion(f32[640,1024]{1,0:T(8,128)} %profile_80.1, s32[1024]{0:T(1024)S(1)} %pad_clamp_fusion), kind=kCustom, calls=%fused_computation.1 | custom fusion | bytes 4196352 | tf_op jit(solution)/shard_map/cond/branch_0_fun/jit(_take)/gather | solution.py:541
  101.6 1.6 broadcast_select_fusion
  103.2 59.3 %spread.1 = (bf16[512,1024]{1,0:T(8,128)(2,1)}, bf16[512,512]{1,0:T(8,128)(2,1)}) custom-call(f32[512,1024]{1,0:T(8,128)} %get-tuple-element.127.run), custom_call_target="tpu_custom_call" | custom-call | tf_op jit(solution)/shard_map/spread/pallas_call | solution.py:463
  162.5 3.1 %tanh_convert_fusion = bf16[1024,512]{1,0:T(8,128)(2,1)} fusion(bf16[512,1024]{1,0:T(8,128)(2,1)} %get-tuple-element.97, bf16[512,512]{1,0:T(8,128)(2,1)} %get-tuple-element.98), kind=kOutput, calls=%fused_computation.52 | convolution fusion | flops 537919488 | bytes 2621440 | tf_op jit(solution)/shard_map/dot_general | solution.py:550
  (13 shorter events, 0.1 us)
